TPU v7x, 32 devices: a whole 2x2x4 slice. The times are simulated.
32 devices in a mesh: group: 2 (over x), tm: 16 (over z, y, core).
Axes of the slice: x: 2, y: 2, z: 4, core: 2. Of those that a mesh axis runs over, the one named last changes fastest.
Arguments:
- noise: float32 [8, 4096], P('group'), parts along dimension 0, may hold values from -6 to 6
- labels: int32 [8], P('group'), parts along dimension 0, may hold values from 0 to 1000
- timesteps: int32 [25], replicated, may hold values from 0 to 399, as said below
- window_start: int32 [1], replicated, may hold values from 0 to 8
- time_weight_in: bfloat16 [256, 768], replicated, may hold values from -0.375 to 0.375
- time_weight_out: bfloat16 [768, 768], replicated, may hold values from -0.21875 to 0.21875
- class_table: bfloat16 [1001, 768], replicated, may hold values from -6 to 6
- patch_weight: bfloat16 [64, 768], replicated, may hold values from -0.75 to 0.75
- query_key_value: bfloat16 [1, 768, 2304], P(None, None, 'tm'), may hold values from -0.21875 to 0.21875
- mix_weight: bfloat16 [1, 768, 768], P(None, None, 'tm'), may hold values from -0.21875 to 0.21875
- expand_weight: bfloat16 [1, 768, 3072], P(None, None, 'tm'), may hold values from -0.21875 to 0.21875
- shrink_weight: bfloat16 [1, 3072, 768], P(None, None, 'tm'), may hold values from -0.109375 to 0.109375
- block_modulation: bfloat16 [1, 768, 4608], P(None, None, 'tm'), may hold values from -0.21875 to 0.21875
- final_modulation: bfloat16 [768, 1536], P(None, 'tm'), may hold values from -0.21875 to 0.21875
- output_weight: bfloat16 [768, 64], replicated, may hold values from -0.21875 to 0.21875
Outputs:
- trajectory: float32 [16, 8, 4096], P('tm', 'group'), parts along dimension 1
There are 2 independent parts, one for each index of `group`. A program takes and returns all parts, laid end to end along the dimension named above; an argument that names none is the same for every part. Nothing has to cross between parts.
Inputs may be any that keep to these rules, and one draw needn't show every extreme that they name: `timesteps`: strictly decreasing; the first entry is 399 and the last is 0.
All inputs are finite; a program needn't handle non-finite values.
Results may differ from a plain program's by a relative error of at most 0.0025.
Values may be sent and summed in bfloat16 or wider, within the bound.
A program may use at most 128 MiB of HBM per device.

v0:
```python
import math

import jax
import jax.numpy as jnp
from jax import lax
from jax.sharding import PartitionSpec as P

HEADS = 12
ITERS = 2
TRAIN_T = 1000


def carried_in(x, axis, combine, identity):
    count, index = (lax.axis_size(axis), lax.axis_index(axis))
    everything = lax.all_gather(x.astype(jnp.bfloat16), axis)
    start = jnp.broadcast_to(jnp.asarray(identity, x.dtype), x.shape)

    def hop(k, before):
        reached = k < index
        new = combine(before, everything[k].astype(x.dtype))
        return jnp.where(reached, new, before)

    return lax.fori_loop(0, count, hop, start)


def layer_norm(values):
    average = jnp.mean(values, axis=-1, keepdims=True)
    centered = values - average
    variance = jnp.mean(centered * centered, axis=-1, keepdims=True)
    return centered / jnp.sqrt(variance + 1e-06)


def position_table(count, width):
    side = math.isqrt(count)
    quarter = width // 4
    omega = 1.0 / 10000.0 ** (jnp.arange(quarter, dtype=jnp.float32) / quarter)
    index = jnp.arange(count, dtype=jnp.int32)
    first = (index // side).astype(jnp.float32)[:, None] * omega[None, :]
    second = (index % side).astype(jnp.float32)[:, None] * omega[None, :]
    return jnp.concatenate(
        [jnp.sin(first), jnp.cos(first), jnp.sin(second), jnp.cos(second)], axis=1
    )


def plan_terms(timesteps, window_start, step_index, train_steps):
    levels = jnp.arange(train_steps, dtype=jnp.float32)
    betas = 0.0001 + (0.02 - 0.0001) * levels / (train_steps - 1)
    alpha_bar = jnp.cumprod(1.0 - betas)
    current = jnp.take(timesteps, window_start[0] + step_index)
    following = jnp.take(timesteps, window_start[0] + step_index + 1)
    bar_current = jnp.take(alpha_bar, current)
    bar_following = jnp.take(alpha_bar, following)
    scale_state = jnp.sqrt(bar_following / bar_current)
    scale_noise = jnp.sqrt(1.0 - bar_following) - scale_state * jnp.sqrt(1.0 - bar_current)
    return (current, scale_state, scale_noise)


def conditioning(current, labels, time_weight_in, time_weight_out, class_table):
    half = time_weight_in.shape[0] // 2
    rates = jnp.exp(-math.log(10000.0) * jnp.arange(half, dtype=jnp.float32) / half)
    angles = current.astype(jnp.float32)[:, None] * rates[None, :]
    features = jnp.concatenate([jnp.cos(angles), jnp.sin(angles)], axis=1).astype(jnp.bfloat16)
    time_hidden = jax.nn.silu(
        jnp.dot(features, time_weight_in, preferred_element_type=jnp.float32)
    ).astype(jnp.bfloat16)
    time_embed = jnp.dot(time_hidden, time_weight_out, preferred_element_type=jnp.float32)
    selector = (
        labels[:, None] == jnp.arange(class_table.shape[0], dtype=jnp.int32)[None, :]
    ).astype(jnp.bfloat16)
    class_embed = jnp.dot(selector, class_table, preferred_element_type=jnp.float32)
    return jax.nn.silu(time_embed[:, None, :] + class_embed[None, :, :]).astype(jnp.bfloat16)


def network(
    states,
    block_terms,
    final_terms,
    patch_weight,
    query_key_value,
    mix_weight,
    expand_weight,
    shrink_weight,
    output_weight,
    heads,
):
    count = states.shape[0]
    patch = patch_weight.shape[0]
    width = patch_weight.shape[1]
    tokens = states.shape[1] // patch
    head_dim = width // heads
    patches = states.reshape(count * tokens, patch).astype(jnp.bfloat16)
    hidden = jnp.dot(patches, patch_weight, preferred_element_type=jnp.float32).reshape(
        count, tokens, width
    )
    hidden = hidden + position_table(tokens, width)[None]
    blocks = block_terms[0].reshape(count, 6, 1, width)
    normed = (layer_norm(hidden) * (1.0 + blocks[:, 1]) + blocks[:, 0]).astype(jnp.bfloat16)
    projected = jnp.dot(
        normed.reshape(count * tokens, width),
        query_key_value[0],
        preferred_element_type=jnp.float32,
    ).astype(jnp.bfloat16)
    projected = projected.reshape(count, tokens, 3, heads, head_dim)
    scores = jnp.einsum(
        "rqhd,rkhd->rhqk",
        projected[:, :, 0],
        projected[:, :, 1],
        preferred_element_type=jnp.float32,
    ) / math.sqrt(head_dim)
    raised = jnp.exp(scores)
    weights = (raised / jnp.sum(raised, axis=-1, keepdims=True)).astype(jnp.bfloat16)
    attended = jnp.einsum(
        "rhqk,rkhd->rqhd", weights, projected[:, :, 2], preferred_element_type=jnp.float32
    ).astype(jnp.bfloat16)
    mixed = jnp.dot(
        attended.reshape(count * tokens, width), mix_weight[0], preferred_element_type=jnp.float32
    )
    hidden = hidden + blocks[:, 2] * mixed.reshape(count, tokens, width)
    normed = (layer_norm(hidden) * (1.0 + blocks[:, 4]) + blocks[:, 3]).astype(jnp.bfloat16)
    expanded = jax.nn.gelu(
        jnp.dot(
            normed.reshape(count * tokens, width),
            expand_weight[0],
            preferred_element_type=jnp.float32,
        ),
        approximate=True,
    ).astype(jnp.bfloat16)
    shrunk = jnp.dot(expanded, shrink_weight[0], preferred_element_type=jnp.float32)
    hidden = hidden + blocks[:, 5] * shrunk.reshape(count, tokens, width)
    final = final_terms.reshape(count, 2, 1, width)
    normed = (layer_norm(hidden) * (1.0 + final[:, 1]) + final[:, 0]).astype(jnp.bfloat16)
    return jnp.dot(
        normed.reshape(count * tokens, width), output_weight, preferred_element_type=jnp.float32
    ).reshape(count, tokens * patch)


def add_terms(earlier, later):
    return earlier + later


def body(
    noise,
    labels,
    timesteps,
    window_start,
    time_weight_in,
    time_weight_out,
    class_table,
    patch_weight,
    query_key_value,
    mix_weight,
    expand_weight,
    shrink_weight,
    block_modulation,
    final_modulation,
    output_weight,
):
    position = lax.axis_index("tm")
    current, scale_state, scale_noise = plan_terms(timesteps, window_start, position[None], TRAIN_T)
    condition = conditioning(current, labels, time_weight_in, time_weight_out, class_table)[0]
    full_query, full_mix, full_expand, full_shrink = (
        lax.all_gather(query_key_value, "tm", axis=2, tiled=True),
        lax.all_gather(mix_weight, "tm", axis=2, tiled=True),
        lax.all_gather(expand_weight, "tm", axis=2, tiled=True),
        lax.all_gather(shrink_weight, "tm", axis=2, tiled=True),
    )
    everyone = lax.all_gather(condition, "tm", axis=0, tiled=True)
    block_part = jnp.einsum(
        "rd,ldc->lrc", everyone, block_modulation, preferred_element_type=jnp.float32
    )
    final_part = jnp.dot(everyone, final_modulation, preferred_element_type=jnp.float32)[None]
    block_terms, final_both = (
        lax.all_to_all(
            block_part.astype(jnp.bfloat16), "tm", split_axis=1, concat_axis=2, tiled=True
        ).astype(block_part.dtype),
        lax.all_to_all(
            final_part.astype(jnp.bfloat16), "tm", split_axis=1, concat_axis=2, tiled=True
        ).astype(final_part.dtype),
    )
    final_terms = final_both[0]
    states = noise
    running = noise
    for sweep in range(ITERS):
        predicted = network(
            states,
            block_terms,
            final_terms,
            patch_weight,
            full_query,
            full_mix,
            full_expand,
            full_shrink,
            output_weight,
            HEADS,
        )
        drift = (scale_state[0] - 1.0) * states + scale_noise[0] * predicted
        before = carried_in(drift, "tm", add_terms, jnp.zeros_like(drift))
        running = before + drift
        states = noise + before
    return (noise + running)[None]


def solution(mesh):
    return jax.shard_map(
        body,
        mesh=mesh,
        in_specs=(
            P("group", None),
            P("group"),
            P(),
            P(),
            P(),
            P(),
            P(),
            P(),
            P(None, None, "tm"),
            P(None, None, "tm"),
            P(None, None, "tm"),
            P(None, None, "tm"),
            P(None, None, "tm"),
            P(None, "tm"),
            P(),
        ),
        out_specs=P("tm", "group", None),
        check_vma=False,
    )
```

profile of v0, /device:TPU:0, one launch (start us, length us, event | category | flops | bytes accessed | tf_op | source)
XLA Modules:
  0.0 295.5 jit_solution(10705091431752967225)
XLA Ops:
  6.6 0.7 all-gather.10.cloned.1.call-update
  7.3 0.7 all-gather.12.cloned.1.call-update
  8.1 0.7 all-gather.14.cloned.1.call-update
  8.8 0.5 all-gather.16.cloned.1.call-update
  10.0 1.4 fusion.87
  12.1 1.2 convolution_reduce_fusion
  13.3 1.6 convolution_reduce_fusion.1
  14.9 0.4 fusion.65
  15.3 23.7 %all-gather.2 = bf16[16,4,768]{2,1,0:T(4,128)(2,1)S(1)} all-gather(bf16[1,4,768]{2,1,0:T(4,128)(2,1)S(1)} %fusion.65), channel_id=1, replica_groups=mesh['group'=2,'tm'=16] {'tm'}, dimensions={0}, use_global_device_ids=true | all-gather | bytes 104448 | tf_op jit(solution)/shard_map/all_gather | solution.py:167
  39.3 0.5 broadcast.360
  39.8 0.7 reduce.7
  40.5 0.7 reshape.443
  41.2 3.5 %all-to-all-start.1 = ((bf16[16,2,192]{2,1,0:T(2,128)(2,1)}), bf16[16,2,192]{2,1,0:T(2,128)(2,1)S(1)}, u32[]{:S(2)}, u32[]{:S(2)}) async-start(bf16[16,2,192]{2,1,0:T(2,128)(2,1)} %reshape.443), calls=%async_computation.1 | async-start | bytes 32768 | tf_op jit(solution)/shard_map/all_to_all | solution.py:176
  44.9 0.3 reduce-window.9
  45.4 0.5 multiply_sine_fusion.1
  46.1 0.7 copy-done.6
  46.7 0.3 fusion.88
  47.1 0.2 multiply_reduce_fusion.5
  47.4 0.3 fusion.50
  48.4 0.7 fusion.86
  50.5 0.9 reduce.6
  51.4 0.7 reshape.441
  52.3 6.0 %all-to-all-start = ((bf16[16,2,576]{2,1,0:T(2,128)(2,1)}), bf16[16,2,576]{2,1,0:T(2,128)(2,1)S(1)}, u32[]{:S(2)}, u32[]{:S(2)}) async-start(bf16[16,2,576]{2,1,0:T(2,128)(2,1)} %reshape.441), calls=%async_computation | async-start | bytes 81920 | tf_op jit(solution)/shard_map/all_to_all | solution.py:173
  58.5 6.4 %all-to-all-done = bf16[16,2,576]{2,1,0:T(2,128)(2,1)S(1)} async-done(((bf16[16,2,576]{2,1,0:T(2,128)(2,1)}), bf16[16,2,576]{2,1,0:T(2,128)(2,1)S(1)}, u32[]{:S(2)}, u32[]{:S(2)}) %all-to-all-start) | async-done | bytes 36896 | tf_op jit(solution)/shard_map/all_to_all | solution.py:173
  65.3 0.6 copy.109
  65.9 0.6 copy.105
  66.5 0.6 copy.106
  67.4 4.3 %convolution_convert_fusion.1 = bf16[256,2304]{1,0:T(8,128)(2,1)} fusion(bf16[256,768]{1,0:T(8,128)(2,1)S(1)} %bitcast.222, bf16[1,768,2304]{1,2,0:T(8,128)(2,1)} %all-gather.10.cloned.1.call-done), kind=kOutput, calls=%fused_computation.13 | convolution fusion | flops 906559488 | bytes 5111808 | tf_op jit(solution)/shard_map/dot_general | solution.py:98
  71.6 1.6 copy.48
  73.2 2.6 reshape.298
  75.8 4.0 %fusion.84 = (bf16[4,64,1,12,64]{1,0,4,3,2:T(4,128)(2,1)}, bf16[4,64,1,12,64]{1,0,4,3,2:T(4,128)(2,1)S(1)}, bf16[4,64,1,12,64]{1,0,4,3,2:T(4,128)(2,1)}) fusion(bf16[4,64,3,12,64]{1,0,4,3,2:T(4,128)(2,1)} %reshape.298), kind=kLoop, calls=%fused_computation.147 | loop fusion | bytes 2359296 | tf_op jit(solution)/shard_map/slice | solution.py:113
  79.8 2.2 copy.79
  82.0 1.3 copy.80
  83.3 3.2 %multiply_exponential_fusion.1 = f32[4,12,64,64]{2,3,1,0:T(8,128)} fusion(bf16[4,64,1,12,64]{4,1,3,0,2:T(8,128)(2,1)} %copy.80, bf16[4,64,1,12,64]{4,1,3,0,2:T(8,128)(2,1)} %copy.79), kind=kOutput, calls=%fused_computation.35 | convolution fusion | flops 25362432 | bytes 1572864 | tf_op jit(solution)/shard_map/rqhd,rkhd->rhqk/dot_general | solution.py:104
  86.4 3.3 %convolution_convert_fusion.3 = bf16[4,12,64,64]{3,2,1,0:T(8,128)(2,1)} fusion(f32[4,12,64,64]{2,3,1,0:T(8,128)} %multiply_exponential_fusion.1, bf16[4,64,1,12,64]{1,0,4,3,2:T(4,128)(2,1)S(1)} %copy-done.11), kind=kOutput, calls=%fused_computation.37 | convolution fusion | flops 25758784 | bytes 1572864 | tf_op jit(solution)/shard_map/rhqk,rkhd->rqhd/dot_general | solution.py:112
  89.8 9.4 %all-gather.12.cloned.1.call-done = bf16[1,768,768]{1,2,0:T(8,128)(2,1)} async-done(((bf16[1,768,48]{1,2,0:T(8,128)(2,1)}), bf16[1,768,768]{1,2,0:T(8,128)(2,1)}) %all-gather.12.cloned.1.call-update) | async-done | bytes 1179664 | tf_op jit(solution)/shard_map/all_gather | solution.py:163
  99.2 2.4 fusion.89
  102.1 51.4 %all-gather.14.cloned.1.call-done = bf16[1,768,3072]{1,2,0:T(8,128)(2,1)} async-done(((bf16[1,768,192]{1,2,0:T(8,128)(2,1)}), bf16[1,768,3072]{1,2,0:T(8,128)(2,1)}) %all-gather.14.cloned.1.call-update) | async-done | bytes 4718608 | tf_op jit(solution)/shard_map/all_gather | solution.py:164
  153.5 5.3 %fusion.19 = bf16[256,3072]{1,0:T(8,128)(2,1)} fusion(bf16[256,768]{1,0:T(8,128)(2,1)S(1)} %bitcast.223, bf16[1,768,3072]{1,2,0:T(8,128)(2,1)} %all-gather.14.cloned.1.call-done), kind=kOutput, calls=%fused_computation.23 | convolution fusion | flops 1215037440 | bytes 6684672 | tf_op jit(solution)/shard_map/dot_general | solution.py:121
  158.8 48.5 %all-gather.16.cloned.1.call-done = bf16[1,3072,768]{1,2,0:T(8,128)(2,1)} async-done(((bf16[1,3072,48]{1,2,0:T(8,128)(2,1)}), bf16[1,3072,768]{1,2,0:T(8,128)(2,1)}) %all-gather.16.cloned.1.call-update) | async-done | bytes 4718608 | tf_op jit(solution)/shard_map/all_gather | solution.py:165
  207.3 4.4 %fusion.90 = (f32[4,64]{1,0:T(4,128)S(1)}, f32[4,64,768]{2,1,0:T(8,128)S(1)}) fusion(f32[4,64,768]{2,1,0:T(8,128)S(1)} %get-tuple-element.282, bf16[4,64,3072]{2,1,0:T(8,128)(2,1)} %bitcast.248, bf16[1,3072,768]{1,2,0:T(8,128)(2,1)} %all-gather.16.cloned.1.call-done, f32[4,768]{1,0:T(4,128)S(1)} %bitcast.243), kind=kOutput, calls=%fused_computation.153 | convolution fusion | flops 1208549120 | bytes 7877632 | tf_op jit(solution)/shard_map/dot_general | solution.py:128
  212.0 0.2 add_convert_fusion.3
  212.3 0.3 convolution_multiply_fusion.3
  212.8 20.6 %all-gather.3 = bf16[16,4,4096]{2,1,0:T(4,128)(2,1)S(1)} all-gather(bf16[1,4,4096]{2,1,0:T(4,128)(2,1)S(1)} %fusion.63), channel_id=2, replica_groups=mesh['group'=2,'tm'=16] {'tm'}, dimensions={0}, use_global_device_ids=true | all-gather | bytes 557056 | tf_op jit(solution)/shard_map/all_gather | solution.py:15
  233.4 1.2 while.32
  234.7 0.6 copy-done.3
  235.4 0.3 fusion.91
  235.7 0.2 multiply_reduce_fusion.2
  236.2 4.2 %convolution_convert_fusion = bf16[256,2304]{1,0:T(8,128)(2,1)} fusion(bf16[256,768]{1,0:T(8,128)(2,1)S(1)} %bitcast.224, bf16[1,768,2304]{1,2,0:T(8,128)(2,1)} %all-gather.10.cloned.1.call-done), kind=kOutput, calls=%fused_computation.12 | convolution fusion | flops 906559488 | bytes 5111808 | tf_op jit(solution)/shard_map/dot_general | solution.py:98
  240.4 1.6 copy.59
  242.0 2.5 reshape.302
  244.5 4.1 %fusion.83 = (bf16[4,64,1,12,64]{1,0,4,3,2:T(4,128)(2,1)}, bf16[4,64,1,12,64]{1,0,4,3,2:T(4,128)(2,1)S(1)}, bf16[4,64,1,12,64]{1,0,4,3,2:T(4,128)(2,1)}) fusion(bf16[4,64,3,12,64]{1,0,4,3,2:T(4,128)(2,1)} %reshape.302), kind=kLoop, calls=%fused_computation.146 | loop fusion | bytes 2359296 | tf_op jit(solution)/shard_map/slice | solution.py:113
  248.6 2.2 copy.82
  250.8 1.3 copy.83
  252.1 3.1 %multiply_exponential_fusion = f32[4,12,64,64]{2,3,1,0:T(8,128)} fusion(bf16[4,64,1,12,64]{4,1,3,0,2:T(8,128)(2,1)} %copy.83, bf16[4,64,1,12,64]{4,1,3,0,2:T(8,128)(2,1)} %copy.82), kind=kOutput, calls=%fused_computation.33 | convolution fusion | flops 25362432 | bytes 1572864 | tf_op jit(solution)/shard_map/rqhd,rkhd->rhqk/dot_general | solution.py:104
  255.2 3.5 %convolution_convert_fusion.2 = bf16[4,12,64,64]{3,2,1,0:T(8,128)(2,1)} fusion(f32[4,12,64,64]{2,3,1,0:T(8,128)} %multiply_exponential_fusion, bf16[4,64,1,12,64]{1,0,4,3,2:T(4,128)(2,1)} %get-tuple-element.255), kind=kOutput, calls=%fused_computation.36 | convolution fusion | flops 25758784 | bytes 1572864 | tf_op jit(solution)/shard_map/rhqk,rkhd->rqhd/dot_general | solution.py:112
  258.7 2.1 fusion.92
  261.3 4.3 %fusion.31 = bf16[256,3072]{1,0:T(8,128)(2,1)S(1)} fusion(bf16[256,768]{1,0:T(8,128)(2,1)S(1)} %bitcast.225, bf16[1,768,3072]{1,2,0:T(8,128)(2,1)} %all-gather.14.cloned.1.call-done), kind=kOutput, calls=%fused_computation.31 | convolution fusion | flops 1215037440 | bytes 6684672 | tf_op jit(solution)/shard_map/dot_general | solution.py:121
  265.6 1.5 fusion.93
  267.4 0.2 add_convert_fusion
  267.7 0.3 convolution_multiply_fusion.2
  268.2 18.9 %all-gather.4 = bf16[16,4,4096]{2,1,0:T(4,128)(2,1)S(1)} all-gather(bf16[1,4,4096]{2,1,0:T(4,128)(2,1)S(1)} %convert_bitcast_fusion), channel_id=3, replica_groups=mesh['group'=2,'tm'=16] {'tm'}, dimensions={0}, use_global_device_ids=true | all-gather | bytes 557056 | tf_op jit(solution)/shard_map/all_gather | solution.py:15
  287.1 1.2 while.33
  288.3 0.7 add_bitcast_fusion
  (161 shorter events, 6.1 us)
Async XLA Ops:
  6.5 8.4 %copy-start = (bf16[1001,768]{1,0:T(8,128)(2,1)S(1)}, bf16[1001,768]{1,0:T(8,128)(2,1)}, u32[]{:S(2)}) copy-start(bf16[1001,768]{1,0:T(8,128)(2,1)} %param.25) | copy-start | bytes 4612612
  6.5 8.4 %copy-start.27 = (s32[4]{0:T(128)S(1)}, s32[4]{0:T(128)}, u32[]{:S(2)}) copy-start(s32[4]{0:T(128)} %param.20) | copy-start | bytes 52
  6.5 32.5 %copy-start.17 = (bf16[768,96]{0,1:T(8,128)(2,1)S(1)}, bf16[768,96]{0,1:T(8,128)(2,1)}, u32[]{:S(2)}) copy-start(bf16[768,96]{0,1:T(8,128)(2,1)} %param.32) | copy-start | bytes 442372
  6.5 38.2 %copy-start.8 = (f32[4,4096]{1,0:T(4,128)S(1)}, f32[4,4096]{1,0:T(4,128)}, u32[]{:S(2)}) copy-start(f32[4,4096]{1,0:T(4,128)} %param.19) | copy-start | bytes 196612
  6.5 60.8 %all-gather.10.cloned.1.call-start = ((), (), s32[]{:S(2)}) async-start(), calls=%async_computation.2 | async-start | bytes 3760128 | tf_op jit(solution)/shard_map/all_gather | solution.py:162
  7.3 91.9 %all-gather.12.cloned.1.call-start = ((), (), s32[]{:S(2)}) async-start(), calls=%async_computation.3 | async-start | bytes 1253376 | tf_op jit(solution)/shard_map/all_gather | solution.py:163
  8.0 145.5 %all-gather.14.cloned.1.call-start = ((), (), s32[]{:S(2)}) async-start(), calls=%async_computation.4 | async-start | bytes 5013504 | tf_op jit(solution)/shard_map/all_gather | solution.py:164
  8.8 198.6 %all-gather.16.cloned.1.call-start = ((), (), s32[]{:S(2)}) async-start(), calls=%async_computation.5 | async-start | bytes 5013504 | tf_op jit(solution)/shard_map/all_gather | solution.py:165
  12.1 34.7 %copy-start.13 = (bf16[64,768]{1,0:T(8,128)(2,1)S(1)}, bf16[64,768]{1,0:T(8,128)(2,1)}, u32[]{:S(2)}) copy-start(bf16[64,768]{1,0:T(8,128)(2,1)} %param.26) | copy-start | bytes 294916
  14.9 32.5 %copy-start.12 = (bf16[1,768,288]{1,2,0:T(8,128)(2,1)S(1)}, bf16[1,768,288]{1,2,0:T(8,128)(2,1)}, u32[]{:S(2)}) copy-start(bf16[1,768,288]{1,2,0:T(8,128)(2,1)} %param.31) | copy-start | bytes 1327108
  41.2 11.0 %all-to-all-start.1 = ((bf16[16,2,192]{2,1,0:T(2,128)(2,1)}), bf16[16,2,192]{2,1,0:T(2,128)(2,1)S(1)}, u32[]{:S(2)}, u32[]{:S(2)}) async-start(bf16[16,2,192]{2,1,0:T(2,128)(2,1)} %reshape.443), calls=%async_computation.1 | async-start | bytes 32768 | tf_op jit(solution)/shard_map/all_to_all | solution.py:176
  46.0 0.7 copy-start.6
  52.3 12.7 %all-to-all-start = ((bf16[16,2,576]{2,1,0:T(2,128)(2,1)}), bf16[16,2,576]{2,1,0:T(2,128)(2,1)S(1)}, u32[]{:S(2)}, u32[]{:S(2)}) async-start(bf16[16,2,576]{2,1,0:T(2,128)(2,1)} %reshape.441), calls=%async_computation | async-start | bytes 81920 | tf_op jit(solution)/shard_map/all_to_all | solution.py:173
  65.3 2.1 copy-start.20
  65.3 2.1 copy-start.22
  83.3 3.2 %copy-start.11 = (bf16[4,64,1,12,64]{1,0,4,3,2:T(4,128)(2,1)S(1)}, bf16[4,64,1,12,64]{1,0,4,3,2:T(4,128)(2,1)}, u32[]{:S(2)}) copy-start(bf16[4,64,1,12,64]{1,0,4,3,2:T(4,128)(2,1)} %get-tuple-element.258) | copy-start | bytes 1179652
  86.4 12.8 %copy-start.24 = (f32[4,1,1,768]{3,0,1,2:T(4,128)S(1)}, f32[4,1,1,768]{3,0,1,2:T(4,128)}, u32[]{:S(2)}) copy-start(f32[4,1,1,768]{3,0,1,2:T(4,128)} %copy.109) | copy-start | bytes 36868
  89.8 12.1 %copy-start.18 = (f32[4,1,1,768]{3,0,1,2:T(4,128)S(1)}, f32[4,1,1,768]{3,0,1,2:T(4,128)}, u32[]{:S(2)}) copy-start(f32[4,1,1,768]{3,0,1,2:T(4,128)} %copy.105) | copy-start | bytes 36868
  153.5 53.8 %copy-start.25 = (f32[4,1,1,768]{3,0,1,2:T(4,128)S(1)}, f32[4,1,1,768]{3,0,1,2:T(4,128)}, u32[]{:S(2)}) copy-start(f32[4,1,1,768]{3,0,1,2:T(4,128)} %copy.106) | copy-start | bytes 36868
  207.3 4.9 %copy-start.15 = (bf16[768,64]{0,1:T(8,128)(2,1)S(1)}, bf16[768,64]{0,1:T(8,128)(2,1)}, u32[]{:S(2)}) copy-start(bf16[768,64]{0,1:T(8,128)(2,1)} %param.33) | copy-start | bytes 294916
  211.7 1.0 copy-start.9
  211.7 21.7 %copy-start.2 = (f32[4,4096]{1,0:T(4,128)S(1)}, f32[4,4096]{1,0:T(4,128)}, u32[]{:S(2)}) copy-start(f32[4,4096]{1,0:T(4,128)} %custom-call) | copy-start | bytes 196612
  211.7 23.6 %copy-start.7 = (f32[64,768]{1,0:T(8,128)S(1)}, f32[64,768]{1,0:T(8,128)}, u32[]{:S(2)}) copy-start(f32[64,768]{1,0:T(8,128)} %copy-done.6) | copy-start | bytes 589828
  211.8 23.6 %copy-start.14 = (bf16[64,768]{1,0:T(8,128)(2,1)S(1)}, bf16[64,768]{1,0:T(8,128)(2,1)}, u32[]{:S(2)}) copy-start(bf16[64,768]{1,0:T(8,128)(2,1)} %param.26) | copy-start | bytes 294916
  212.2 23.7 %copy-start.21 = (f32[4,1,1,768]{3,0,1,2:T(4,128)S(1)}, f32[4,1,1,768]{3,0,1,2:T(4,128)}, u32[]{:S(2)}) copy-start(f32[4,1,1,768]{3,0,1,2:T(4,128)} %copy-done.20) | copy-start | bytes 36868
  212.3 23.7 %copy-start.23 = (f32[4,1,1,768]{3,0,1,2:T(4,128)S(1)}, f32[4,1,1,768]{3,0,1,2:T(4,128)}, u32[]{:S(2)}) copy-start(f32[4,1,1,768]{3,0,1,2:T(4,128)} %copy-done.22) | copy-start | bytes 36868
  234.6 0.6 copy-start.3
  255.2 3.5 %copy-start.1 = (bf16[1,768,768]{1,2,0:T(8,128)(2,1)S(1)}, bf16[1,768,768]{1,2,0:T(8,128)(2,1)}, u32[]{:S(2)}) copy-start(bf16[1,768,768]{1,2,0:T(8,128)(2,1)} %all-gather.12.cloned.1.call-done) | copy-start | bytes 3538948
  258.7 2.3 copy-start.19
  261.1 4.5 %slice-start = ((s8[4718592]{0:T(1024)(128)(4,1)}), s8[4194304]{0:T(1024)(128)(4,1)S(1)}, s32[]{:S(2)}) async-start(s8[4718592]{0:T(1024)(128)(4,1)} %bitcast.246), calls=%async_computation.6 | async-start | bytes 8388608
  261.3 4.3 %copy-start.26 = (f32[4,1,1,768]{3,0,1,2:T(4,128)S(1)}, f32[4,1,1,768]{3,0,1,2:T(4,128)}, u32[]{:S(2)}) copy-start(f32[4,1,1,768]{3,0,1,2:T(4,128)} %copy.106) | copy-start | bytes 36868
  261.3 4.3 %slice-start.1 = ((s8[4718592]{0:T(1024)(128)(4,1)}), s8[524288]{0:T(1024)(128)(4,1)S(1)}, s32[]{:S(2)}) async-start(s8[4718592]{0:T(1024)(128)(4,1)} %bitcast.246), calls=%async_computation.7 | async-start | bytes 1048576
  265.6 2.0 copy-start.16
  267.1 1.0 copy-start.4
  267.2 1.0 copy-start.10
  267.2 19.9 %copy-start.5 = (f32[4,4096]{1,0:T(4,128)S(1)}, f32[4,4096]{1,0:T(4,128)}, u32[]{:S(2)}) copy-start(f32[4,4096]{1,0:T(4,128)} %custom-call.1) | copy-start | bytes 196612
Sparse Core Ops, SparseCore 0:
  9.6 50.2 all-gather.9
  62.2 36.9 all-gather.11
  101.5 51.9 all-gather.13
  155.6 51.6 all-gather.15
where the time goes:
time: 296 us; the launch traced here: 295 us
  waiting for transfers between devices  118 us (40%)
  blocking collectives  63.2 us (21%)
  matrix products  46.3 us (16%)
  local copies, waits for them, and re-layouts  31.9 us (11%)
  between operations  17.4 us (6%)
  starting transfers between devices  9.62 us (3%)
  other arithmetic  8.2 us (3%)
    all_gather x1, waiting for transfers between devices, body(): lax.all_gather(expand_weight, 'tm', axis=2, tiled=True)  51.4 us
    all_gather x1, waiting for transfers between devices, body(): lax.all_gather(shrink_weight, 'tm', axis=2, tiled=True)  48.5 us
    all_gather x2, blocking collectives, carried_in(): everything = lax.all_gather(x.astype(jnp.bfloat16), axis)  39.5 us
    all_gather x1, blocking collectives, body(): everyone = lax.all_gather(condition, 'tm', axis=0, tiled=True)  23.7 us
    unnamed x78, local copies, waits for them, and re-layouts  12.4 us
    dot_general x2, matrix products, network(): jnp.dot(normed.reshape(count * tokens, width), expand_weight[0], preferre...  9.56 us
    all_gather x1, waiting for transfers between devices, body(): lax.all_gather(mix_weight, 'tm', axis=2, tiled=True)  9.4 us
    dot_general x2, matrix products, network(): jnp.dot(normed.reshape(count * tokens, width), query_key_value[0], prefer...  8.47 us
  transfers between devices with their start and end apart: 6, of which 4 were waited for; matrix products, arithmetic and copies ran while one was open for 15% of the time, Pallas kernels for 0%

commit v1 on v0

--- a/solution.py
+++ b/solution.py
@@ -1,8 +1,12 @@
+import functools
 import math
 
 import jax
 import jax.numpy as jnp
+import numpy as np
 from jax import lax
+from jax.experimental import pallas as pl
+from jax.experimental.pallas import tpu as pltpu
 from jax.sharding import PartitionSpec as P
 
 HEADS = 12
@@ -138,7 +142,7 @@
     return earlier + later
 
 
-def body(
+def gathered_body(
     noise,
     labels,
     timesteps,
@@ -200,7 +204,494 @@
     return (noise + running)[None]
 
 
+PLANE = 4
+PAD = 8
+ROW_TILE = 256
+
+
+def alpha_table():
+    levels = np.arange(TRAIN_T, dtype=np.float64)
+    return np.cumprod(1.0 - (0.0001 + (0.02 - 0.0001) * levels / (TRAIN_T - 1))).astype(np.float32)
+
+
+def position_columns(count, width):
+    side = math.isqrt(count)
+    quarter = width // 4
+    omega = 1.0 / 10000.0 ** (np.arange(quarter, dtype=np.float64) / quarter)
+    index = np.arange(count)
+    first = (index // side)[:, None] * omega[None, :]
+    second = (index % side)[:, None] * omega[None, :]
+    table = np.concatenate([np.sin(first), np.cos(first), np.sin(second), np.cos(second)], axis=1)
+    return table.T.astype(np.float32)
+
+
+def matmul(a, b):
+    return jnp.dot(a, b, preferred_element_type=jnp.float32)
+
+
+def kernel(
+    n,
+    samples,
+    plan_ref,
+    start_ref,
+    alpha_ref,
+    noise_ref,
+    class_ref,
+    tin_ref,
+    tout_ref,
+    modw_ref,
+    patch_ref,
+    outw_ref,
+    pos_ref,
+    q_ref,
+    m_ref,
+    e_ref,
+    s_ref,
+    out_ref,
+    q_full,
+    m_full,
+    e_full,
+    s_full,
+    terms,
+    hidden,
+    projected,
+    attended,
+    expanded,
+    mods_send,
+    mods_recv,
+    drift_send,
+    drift_recv,
+    total_send,
+    total_recv,
+    ring_recv,
+    ring_send,
+    x_recv,
+    x_send,
+    mate_recv,
+    mate_send,
+    local_sem,
+    mods_sems,
+    plane_sems,
+    total_rsem,
+    total_ssem,
+):
+    me, g = lax.axis_index("tm"), lax.axis_index("group")
+    chips = n // 2
+    half = chips // 2
+    chip, core = lax.div(me, 2), lax.rem(me, 2)
+    odd = lax.rem(chip, 2)
+    pos = (1 - odd) * lax.div(chip, 2) + odd * (chips - 1 - lax.div(chip, 2))
+
+    def device_at(place):
+        place = lax.rem(place + chips, chips)
+        upper = lax.div(place, half)
+        where = (1 - upper) * (2 * place) + upper * (2 * (chips - 1 - place) + 1)
+        return where * 2 + core
+
+    right, left = {"tm": device_at(pos + 1)}, {"tm": device_at(pos - 1)}
+    mate = {"tm": me + 1 - 2 * core}
+    side = lax.rem(g, 2)
+    xmate = {"group": g + 1 - 2 * side}
+    fulls, shards = (q_full, m_full, e_full, s_full), (q_ref, m_ref, e_ref, s_ref)
+
+    barrier = pltpu.get_barrier_semaphore()
+    for off in range(1, n):
+        pl.semaphore_signal(barrier, inc=1, device_id={"tm": lax.rem(me + off, n)}, device_id_type=pl.DeviceIdType.MESH)
+    pl.semaphore_signal(barrier, inc=1, device_id=xmate, device_id_type=pl.DeviceIdType.MESH)
+    pl.semaphore_wait(barrier, n)
+
+    def send(src, dst, ssem, rsem, target):
+        return pltpu.make_async_remote_copy(
+            src_ref=src, dst_ref=dst, send_sem=ssem, recv_sem=rsem,
+            device_id=target, device_id_type=pl.DeviceIdType.MESH,
+        )
+
+    def third(m):
+        return shards[m].shape[0] // 3
+
+    def part(m, owner, off, count):
+        rows = shards[m].shape[0]
+        return fulls[m].at[pl.ds(pl.multiple_of(owner * rows + off, 16), count)]
+
+    def own(m, off, count):
+        return shards[m].at[pl.ds(pl.multiple_of(off, 16), count)]
+
+    def begin(m):
+        t = third(m)
+        off = side * t
+        for way, target in ((0, right), (1, left)):
+            send(own(m, off, 2 * t), part(m, me, off, 2 * t), ring_send.at[m], ring_recv.at[m, way, 0], target).start()
+        send(shards[m], part(m, me, 0, 3 * t), mate_send.at[m], mate_recv.at[m], mate).start()
+        pltpu.make_async_copy(shards[m], part(m, me, 0, 3 * t), local_sem.at[m]).start()
+
+    def slab(m, way, hop):
+        t = third(m)
+        if hop < half:
+            return side * t, 2 * t
+        return side * t + way * t, t
+
+    def take(m, hop):
+        t = third(m)
+        for way, target in ((0, right), (1, left)):
+            owner = device_at(pos - hop) if way == 0 else device_at(pos + hop)
+            off, count = slab(m, way, hop)
+            here = part(m, owner, off, count)
+            send(here, here, ring_send.at[m], ring_recv.at[m, way, hop - 1], target).wait_recv()
+            if hop < half:
+                onward = part(m, owner, *slab(m, way, hop + 1))
+                send(onward, onward, ring_send.at[m], ring_recv.at[m, way, hop], target).start()
+                across = part(m, owner, side * 2 * t, t)
+                send(across, across, x_send.at[m], x_recv.at[m, 2 * (hop - 1) + way], xmate).start()
+            send(here, here, mate_send.at[m], mate_recv.at[m], mate).start()
+        if hop == half:
+            across = part(m, device_at(pos + half), side * 2 * t, t)
+            send(across, across, x_send.at[m], x_recv.at[m, 2 * (half - 1)], xmate).start()
+
+    def take_across(m, hop):
+        t = third(m)
+        for way in ((0, 1) if hop < half else (0,)):
+            owner = device_at(pos - hop) if way == 0 else device_at(pos + hop)
+            here = part(m, owner, (1 - side) * 2 * t, t)
+            send(here, here, x_send.at[m], x_recv.at[m, 2 * (hop - 1) + way], xmate).wait_recv()
+            send(here, here, mate_send.at[m], mate_recv.at[m], mate).start()
+
+    def settle(m):
+        rows = shards[m].shape[0]
+        everything = fulls[m].at[pl.ds(0, chips * rows)]
+        send(everything, everything, mate_send.at[m], mate_recv.at[m], mate).wait_recv()
+        pltpu.make_async_copy(shards[m], part(m, me, 0, rows), local_sem.at[m]).wait()
+
+    def drain(m):
+        t = third(m)
+        for sem, count in ((ring_send, (4 * half - 2) * t), (x_send, (2 * half - 1) * t), (mate_send, 6 * half * t)):
+            whole = fulls[m].at[pl.ds(0, count)]
+            send(whole, whole, sem.at[m], mate_recv.at[m], mate).wait_send()
+
+    begin(0)
+
+    width = tin_ref.shape[1]
+    freq = tin_ref.shape[0]
+    first = start_ref[0]
+    step_of = lax.broadcasted_iota(jnp.int32, (n * PAD, freq // 2), 0) // PAD
+    current = jnp.zeros((n * PAD, freq // 2), jnp.float32)
+    for j in range(n):
+        current = jnp.where(step_of == j, plan_ref[first + j].astype(jnp.float32), current)
+    lane = lax.broadcasted_iota(jnp.int32, (n * PAD, freq // 2), 1).astype(jnp.float32)
+    angles = current * jnp.exp(-math.log(10000.0) * lane / (freq // 2))
+    features = jnp.concatenate([jnp.cos(angles), jnp.sin(angles)], axis=1).astype(jnp.bfloat16)
+    time_hidden = jax.nn.silu(matmul(features, tin_ref[...])).astype(jnp.bfloat16)
+    classes = class_ref[...].astype(jnp.float32)
+    summed = matmul(time_hidden, tout_ref[...]) + jnp.concatenate([classes] * n, axis=0)
+    condition = jax.nn.silu(summed).astype(jnp.bfloat16)
+    columns = modw_ref.shape[1]
+    mods_send[...] = matmul(condition, modw_ref[...]).reshape(n, PAD, columns)
+    mods_recv[me] = mods_send[me]
+    for off in range(1, n):
+        peer = lax.rem(me + off, n)
+        send(mods_send.at[peer], mods_recv.at[me], mods_sems.at[0], mods_sems.at[1], {"tm": peer}).start()
+
+    begin(1)
+    tokens = noise_ref.shape[1]
+    per = tokens // samples
+
+    current_t, following_t = plan_ref[first + me], plan_ref[first + me + 1]
+    shape = (1, tokens)
+    bar_current = jnp.full(shape, alpha_ref[current_t], jnp.float32)
+    bar_following = jnp.full(shape, alpha_ref[following_t], jnp.float32)
+    scale_state = jnp.sqrt(bar_following / bar_current)
+    scale_noise = jnp.sqrt(1.0 - bar_following) - scale_state * jnp.sqrt(1.0 - bar_current)
+
+    def spread_terms():
+        for way in (0, 1):
+            some = mods_recv.at[pl.ds(0, n - 1)]
+            copy = send(some, some, mods_sems.at[0], mods_sems.at[1], mate)
+            copy.wait_send() if way == 0 else copy.wait_recv()
+        flat = mods_recv[...].reshape(n * PAD, columns)
+        turned = jnp.transpose(flat).astype(jnp.bfloat16)
+        block = columns * 3 // 4
+        last = columns - block
+        row = lax.broadcasted_iota(jnp.int32, (n * PAD, tokens), 0)
+        wanted = lax.broadcasted_iota(jnp.int32, (n * PAD, tokens), 1) // per
+        for d in range(n):
+            pick = (row == d * PAD + wanted).astype(jnp.bfloat16)
+            both = matmul(turned, pick)
+            terms[pl.ds(d * block, block)] = both[:block]
+            terms[pl.ds(n * block + d * last, last)] = both[block:]
+
+    def term(k):
+        return terms[pl.ds(k * width, width)]
+
+    def normal(shift, scale):
+        h = hidden[...]
+        average = jnp.mean(h, axis=0, keepdims=True)
+        centered = h - average
+        variance = jnp.mean(centered * centered, axis=0, keepdims=True)
+        return (centered / jnp.sqrt(variance + 1e-06) * (1.0 + term(scale)) + term(shift)).astype(jnp.bfloat16)
+
+    def tiles(count, action):
+        def step(i, _):
+            action(pl.ds(pl.multiple_of(i * ROW_TILE, ROW_TILE), ROW_TILE), i)
+            return 0
+
+        lax.fori_loop(0, count // ROW_TILE, step, 0)
+
+    def embed(states):
+        pos2 = jnp.concatenate([pos_ref[...]] * (tokens // pos_ref.shape[1]), axis=1)
+        hidden[...] = matmul(patch_ref[...], states.astype(jnp.bfloat16)) + pos2
+
+    def project():
+        normed = normal(0, 1)
+
+        def action(rows, i):
+            projected[rows] = matmul(q_full[rows], normed).astype(jnp.bfloat16)
+
+        tiles(3 * width, action)
+
+    head_dim = width // HEADS
+    lanes = 128
+    same = (
+        lax.broadcasted_iota(jnp.int32, (lanes, lanes), 0) // per
+        == lax.broadcasted_iota(jnp.int32, (lanes, lanes), 1) // per
+    )
+
+    def attend():
+        def one(i, _):
+            base = pl.multiple_of(i * head_dim, head_dim)
+            for p in range(tokens // lanes):
+                cols = pl.ds(p * lanes, lanes)
+                q = projected[pl.ds(base, head_dim), cols]
+                k = projected[pl.ds(base + width, head_dim), cols]
+                v = projected[pl.ds(base + 2 * width, head_dim), cols]
+                scores = lax.dot_general(k, q, (((0,), (0,)), ((), ())), preferred_element_type=jnp.float32) / math.sqrt(head_dim)
+                raised = jnp.exp(jnp.where(same, scores, -jnp.inf))
+                weights = (raised / jnp.sum(raised, axis=0, keepdims=True)).astype(jnp.bfloat16)
+                attended[pl.ds(base, head_dim), cols] = matmul(v, weights).astype(jnp.bfloat16)
+            return 0
+
+        lax.fori_loop(0, HEADS, one, 0, unroll=2)
+
+    def mix():
+        a = attended[...]
+
+        def action(rows, i):
+            gate = terms[pl.ds(pl.multiple_of(2 * width + i * ROW_TILE, ROW_TILE), ROW_TILE)]
+            hidden[rows] += gate * matmul(m_full[rows], a)
+
+        tiles(width, action)
+
+    def expand():
+        normed = normal(3, 4)
+
+        def action(rows, i):
+            expanded[rows] = jax.nn.gelu(matmul(e_full[rows], normed), approximate=True).astype(jnp.bfloat16)
+
+        tiles(expanded.shape[0], action)
+
+    def shrink():
+        def action(rows, i):
+            gate = terms[pl.ds(pl.multiple_of(5 * width + i * ROW_TILE, ROW_TILE), ROW_TILE)]
+            hidden[rows] += gate * matmul(s_full[rows], expanded[...])
+
+        tiles(width, action)
+
+    def drift_of(states):
+        predicted = matmul(outw_ref[...], normal(6, 7))
+        return (scale_state - 1.0) * states + scale_noise * predicted
+
+    planes = n // PLANE
+    plane, spot = lax.div(me, PLANE), lax.rem(me, PLANE)
+
+    def earlier(sweep, drift):
+        mine = drift.astype(jnp.bfloat16)
+        drift_send[sweep] = mine
+        drift_recv[sweep, spot] = mine
+        for off in range(1, PLANE):
+            peer = plane * PLANE + lax.rem(spot + off, PLANE)
+            send(drift_send.at[sweep], drift_recv.at[sweep, spot], plane_sems.at[sweep, 0], plane_sems.at[sweep, 1], {"tm": peer}).start()
+        some = drift_recv.at[sweep, pl.ds(0, PLANE - 1)]
+        send(some, some, plane_sems.at[sweep, 0], plane_sems.at[sweep, 1], mate).wait_recv()
+        pieces = [drift_recv[sweep, i].astype(jnp.float32) for i in range(PLANE)]
+        total_send[sweep] = functools.reduce(lambda a, b: a + b, pieces).astype(jnp.bfloat16)
+        for b in range(1, planes):
+            @pl.when(plane < b)
+            def _():
+                send(total_send.at[sweep], total_recv.at[sweep, plane], total_ssem.at[sweep, b], total_rsem.at[sweep, plane], {"tm": b * PLANE + spot}).start()
+
+        before = jnp.zeros_like(drift)
+        for i in range(PLANE - 1):
+            before = before + jnp.where(i < spot, pieces[i], 0.0)
+        out_ref[...] = before
+        for b in range(planes - 1):
+            @pl.when(b < plane)
+            def _():
+                slot = total_recv.at[sweep, b]
+                send(slot, slot, total_ssem.at[sweep, b], total_rsem.at[sweep, b], mate).wait_recv()
+                out_ref[...] += total_recv[sweep, b].astype(jnp.float32)
+
+        send(some, some, plane_sems.at[sweep, 0], plane_sems.at[sweep, 1], mate).wait_send()
+        for b in range(1, planes):
+            @pl.when(plane < b)
+            def _():
+                slot = total_send.at[sweep]
+                send(slot, slot, total_ssem.at[sweep, b], total_rsem.at[sweep, 0], mate).wait_send()
+
+        return out_ref[...]
+
+    def arrive(m):
+        for hop in range(1, half + 1):
+            take(m, hop)
+            if hop > 1:
+                take_across(m, hop - 1)
+        take_across(m, half)
+        settle(m)
+
+    noise = noise_ref[...]
+    states = noise
+    embed(states)
+    begin(2)
+    spread_terms()
+    arrive(0)
+    begin(3)
+    project()
+    attend()
+    arrive(1)
+    mix()
+    arrive(2)
+    expand()
+    arrive(3)
+    shrink()
+    drift = drift_of(states)
+    states = noise + earlier(0, drift)
+    for m in range(4):
+        drain(m)
+    for sweep in range(1, ITERS):
+        embed(states)
+        project()
+        attend()
+        mix()
+        expand()
+        shrink()
+        drift = drift_of(states)
+        before = earlier(sweep, drift)
+        states = noise + before
+    out_ref[...] = states + drift
+
+
+def fused_body(
+    n,
+    noise,
+    labels,
+    timesteps,
+    window_start,
+    time_weight_in,
+    time_weight_out,
+    class_table,
+    patch_weight,
+    query_key_value,
+    mix_weight,
+    expand_weight,
+    shrink_weight,
+    block_modulation,
+    final_modulation,
+    output_weight,
+):
+    samples, latent = noise.shape
+    patch, width = patch_weight.shape
+    count = latent // patch
+    tokens = samples * count
+    hidden_units = shrink_weight.shape[1]
+    noise_columns = noise.reshape(tokens, patch).T
+    classes = jnp.take(class_table, labels, axis=0, mode="clip")
+    classes = jnp.concatenate([classes] * (PAD // samples), axis=0)
+    modulation = jnp.concatenate([block_modulation[0], final_modulation], axis=1)
+    columns = modulation.shape[1]
+    shards = [w[0].T for w in (query_key_value, mix_weight, expand_weight, shrink_weight)]
+    table = position_columns(count, width)
+    positions = np.concatenate([table] * (128 // count), axis=1)
+    half = n // 4
+    vmem, smem = pl.BlockSpec(memory_space=pltpu.VMEM), pl.BlockSpec(memory_space=pltpu.SMEM)
+    dma = pltpu.SemaphoreType.DMA
+    bf16, f32 = jnp.bfloat16, jnp.float32
+    out = pl.pallas_call(
+        functools.partial(kernel, n, samples),
+        out_shape=jax.ShapeDtypeStruct((patch, tokens), f32),
+        in_specs=[smem] * 3 + [vmem] * 12,
+        out_specs=vmem,
+        scratch_shapes=[pltpu.VMEM((s.shape[0] * n, s.shape[1]), bf16) for s in shards]
+        + [
+            pltpu.VMEM((8 * width, tokens), f32),
+            pltpu.VMEM((width, tokens), f32),
+            pltpu.VMEM((3 * width, tokens), bf16),
+            pltpu.VMEM((width, tokens), bf16),
+            pltpu.VMEM((hidden_units, tokens), bf16),
+            pltpu.VMEM((n, PAD, columns), f32),
+            pltpu.VMEM((n, PAD, columns), f32),
+            pltpu.VMEM((ITERS, patch, tokens), bf16),
+            pltpu.VMEM((ITERS, PLANE, patch, tokens), bf16),
+            pltpu.VMEM((ITERS, patch, tokens), bf16),
+            pltpu.VMEM((ITERS, n // PLANE, patch, tokens), bf16),
+            dma((4, 2, half)),
+            dma((4,)),
+            dma((4, 2 * half - 1)),
+            dma((4,)),
+            dma((4,)),
+            dma((4,)),
+            dma((4,)),
+            dma((2,)),
+            dma((ITERS, 2)),
+            dma((ITERS, n // PLANE)),
+            dma((ITERS, n // PLANE)),
+        ],
+        compiler_params=pltpu.CompilerParams(
+            collective_id=0, has_side_effects=True, vmem_limit_bytes=60 * 1024 * 1024
+        ),
+    )(
+        timesteps,
+        window_start,
+        jnp.asarray(alpha_table()),
+        noise_columns,
+        classes,
+        time_weight_in,
+        time_weight_out,
+        modulation,
+        patch_weight.T,
+        output_weight.T,
+        jnp.asarray(positions),
+        *shards,
+    )
+    return out.T.reshape(1, samples, latent)
+
+
+def fits(n, groups, args):
+    rows = [args[i].shape[-1] // n for i in (8, 9, 10, 11)]
+    columns = (args[12].shape[-1] + args[13].shape[-1]) // n
+    samples = args[0].shape[0] // groups
+    count = args[0].shape[1] // args[7].shape[0]
+    return (
+        groups % 2 == 0
+        and n % 8 == 0
+        and all(r % 48 == 0 for r in rows)
+        and columns % 128 == 0
+        and PAD % samples == 0
+        and 128 % count == 0
+        and samples * count % 128 == 0
+        and args[12].shape[-1] == 3 * args[13].shape[-1]
+        and args[10].shape[-1] % ROW_TILE == 0
+        and args[9].shape[-1] % ROW_TILE == 0
+    )
+
+
 def solution(mesh):
+    n, groups = mesh.shape["tm"], mesh.shape["group"]
+
+    def run(*args):
+        chosen = functools.partial(fused_body, n) if fits(n, groups, args) else gathered_body
+        return shard(chosen, mesh)(*args)
+
+    return run
+
+
+def shard(body, mesh):
     return jax.shard_map(
         body,
         mesh=mesh,

time: 296 us -> 138 us (0.47)
  Pallas kernels: 0 us -> 129 us
  waiting for transfers between devices: 118 us -> 0 us
  blocking collectives: 63.2 us -> 0 us
  matrix products: 46.3 us -> 0 us
  local copies, waits for them, and re-layouts: 31.9 us -> 6.46 us
  between operations: 17.4 us -> 0.7 us
  starting transfers between devices: 9.62 us -> 0 us
  other arithmetic: 8.2 us -> 1.57 us
    pallas_call x0 -> x1, Pallas kernels: none -> 129 us  [fused_body(): pl.pallas_call(functools.partial(kernel, n, samples), out_shape=jax.Shape...]
    all_gather x4 -> x0, waiting for transfers between devices: 109 us -> none  [the longest x1 51.4 us: body(): lax.all_gather(expand_weight, 'tm', axis=2, tiled=True)]
    all_gather x3 -> x0, blocking collectives: 63.2 us -> none  [the longest x2 39.5 us: carried_in(): everything = lax.all_gather(x.astype(jnp.bfloat16), axis)]
    dot_general x21 -> x0, matrix products: 46.3 us -> none  [the longest x2 9.56 us: network(): jnp.dot(normed.reshape(count * tokens, width), expand_weight[0], preferre...]
    all_to_all x2 -> x0, starting transfers between devices: 9.47 us -> none  [the longest x1 5.99 us: body(): lax.all_to_all(block_part.astype(jnp.bfloat16), 'tm', split_axis=1, conca...]
    unnamed x78 -> x11, local copies, waits for them, and re-layouts: 12.4 us -> 3.38 us
    slice x3 -> x0, local copies, waits for them, and re-layouts: 8.25 us -> none  [the longest x2 8.18 us: network(): projected[:, :, 2]]
    all_to_all x2 -> x0, waiting for transfers between devices: 6.4 us -> none  [the longest x1 6.39 us: body(): lax.all_to_all(block_part.astype(jnp.bfloat16), 'tm', split_axis=1, conca...]
  transfers between devices with their start and end apart: 6 -> 0, of which waited for: 4 -> 0; matrix products, arithmetic and copies ran while one was open for 15% -> 0% of each run, Pallas kernels for 0% -> 0%
where the time goes in v1:
time: 138 us
  Pallas kernels  129 us (93%)
  local copies, waits for them, and re-layouts  6.46 us (5%)
  other arithmetic  1.57 us (1%)
    pallas_call x1, Pallas kernels, fused_body(): pl.pallas_call(functools.partial(kernel, n, samples), out_shape=jax.Shape...  129 us
    unnamed x11, local copies, waits for them, and re-layouts  3.38 us

profile of v1, /device:TPU:0, one launch (start us, length us, event | category | flops | bytes accessed | tf_op | source)
XLA Modules:
  0.0 137.9 jit_solution(14170113921754379630)
XLA Ops:
  0.0 0.0 copy-start
  0.0 0.0 copy-start.2
  0.0 1.4 %copy.22 = bf16[1,768,288]{2,1,0:T(8,128)(2,1)S(1)} copy(bf16[1,768,288]{1,2,0:T(8,128)(2,1)} %param.29) | data formatting | bytes 884736 | tf_op args[12]
  1.4 0.0 copy-start.1
  1.5 0.0 copy-start.3
  1.5 1.1 copy.23
  2.6 1.0 pad_maximum_fusion.modw_ref
  3.5 0.0 copy-done.2
  3.5 0.1 reshape.6
  3.7 0.7 copy.21
  4.4 0.0 copy-done.1
  4.4 0.8 copy.24
  5.2 0.0 copy-done.3
  5.2 0.0 copy-done
  5.2 0.6 gather_fusion
  5.8 0.6 pad_maximum_fusion.1.class_ref
  7.0 129.2 %shard_map.163 = f32[64,256]{1,0:T(8,128)} custom-call(s32[25]{0:T(128)} %plan_ref.1, s32[1]{0:T(128)S(6)} %copy.26.start_ref, f32[1000]{0:T(1024)} %constant.4.clone.alpha_ref, f32[64,256]{1,0:T(8,128)} %bitcast.21, bf16[8,768]{1,0:T(8,128)(2,1)} %pad_maximum_fusion.1.class_ref, bf16[256,768]{1,0:T(8,128)(2,1)} %tin_ref.1, bf16[768,768]{1,0:T(8,128)(2,1)} %tout_ref.1, ...), custom_call_target="tpu_custom_call" | custom-call | tf_op jit(solution)/shard_map/pallas_call | solution.py:615
  136.2 0.9 copy.25
  137.2 0.7 reshape.7
  (1 shorter events, 0.0 us)
Async XLA Ops:
  0.0 5.2 %copy-start = (bf16[1001,768]{1,0:T(8,128)(2,1)S(1)}, bf16[1001,768]{1,0:T(8,128)(2,1)}, u32[]{:S(2)}) copy-start(bf16[1001,768]{1,0:T(8,128)(2,1)} %param.23) | copy-start | bytes 4612612
  0.0 3.5 %copy-start.2 = (f32[4,4096]{1,0:T(4,128)S(1)}, f32[4,4096]{1,0:T(4,128)}, u32[]{:S(2)}) copy-start(f32[4,4096]{1,0:T(4,128)} %param.17) | copy-start | bytes 196612
  1.4 2.9 %copy-start.1 = (bf16[64,768]{1,0:T(8,128)(2,1)S(1)}, bf16[64,768]{1,0:T(8,128)(2,1)}, u32[]{:S(2)}) copy-start(bf16[64,768]{1,0:T(8,128)(2,1)} %param.24) | copy-start | bytes 294916
  1.5 3.7 %copy-start.3 = (s32[4]{0:T(128)S(1)}, s32[4]{0:T(128)}, u32[]{:S(2)}) copy-start(s32[4]{0:T(128)} %param.18) | copy-start | bytes 52

commit v2 on v1

--- a/solution.py
+++ b/solution.py
@@ -229,6 +229,14 @@
     return jnp.dot(a, b, preferred_element_type=jnp.float32)
 
 
+def matmul_turned(a, b):
+    return lax.dot_general(a, b, (((1,), (1,)), ((), ())), preferred_element_type=jnp.float32)
+
+
+def turned_matmul(a, b):
+    return lax.dot_general(a, b, (((0,), (0,)), ((), ())), preferred_element_type=jnp.float32)
+
+
 def kernel(
     n,
     samples,
@@ -240,6 +248,7 @@
     tin_ref,
     tout_ref,
     modw_ref,
+    finalw_ref,
     patch_ref,
     outw_ref,
     pos_ref,
@@ -274,6 +283,7 @@
     plane_sems,
     total_rsem,
     total_ssem,
+    before_ref,
 ):
     me, g = lax.axis_index("tm"), lax.axis_index("group")
     chips = n // 2
@@ -330,7 +340,13 @@
             return side * t, 2 * t
         return side * t + way * t, t
 
-    def take(m, hop):
+    def onward(m, hop):
+        for way, target in ((0, right), (1, left)):
+            owner = device_at(pos - hop) if way == 0 else device_at(pos + hop)
+            rows = part(m, owner, *slab(m, way, hop + 1))
+            send(rows, rows, ring_send.at[m], ring_recv.at[m, way, hop], target).start()
+
+    def take(m, hop, pass_on=True):
         t = third(m)
         for way, target in ((0, right), (1, left)):
             owner = device_at(pos - hop) if way == 0 else device_at(pos + hop)
@@ -338,8 +354,9 @@
             here = part(m, owner, off, count)
             send(here, here, ring_send.at[m], ring_recv.at[m, way, hop - 1], target).wait_recv()
             if hop < half:
-                onward = part(m, owner, *slab(m, way, hop + 1))
-                send(onward, onward, ring_send.at[m], ring_recv.at[m, way, hop], target).start()
+                if pass_on:
+                    rows = part(m, owner, *slab(m, way, hop + 1))
+                    send(rows, rows, ring_send.at[m], ring_recv.at[m, way, hop], target).start()
                 across = part(m, owner, side * 2 * t, t)
                 send(across, across, x_send.at[m], x_recv.at[m, 2 * (hop - 1) + way], xmate).start()
             send(here, here, mate_send.at[m], mate_recv.at[m], mate).start()
@@ -367,7 +384,8 @@
             whole = fulls[m].at[pl.ds(0, count)]
             send(whole, whole, sem.at[m], mate_recv.at[m], mate).wait_send()
 
-    begin(0)
+    for m in range(4):
+        begin(m)
 
     width = tin_ref.shape[1]
     freq = tin_ref.shape[0]
@@ -380,18 +398,19 @@
     angles = current * jnp.exp(-math.log(10000.0) * lane / (freq // 2))
     features = jnp.concatenate([jnp.cos(angles), jnp.sin(angles)], axis=1).astype(jnp.bfloat16)
     time_hidden = jax.nn.silu(matmul(features, tin_ref[...])).astype(jnp.bfloat16)
-    classes = class_ref[...].astype(jnp.float32)
+    classes = jnp.concatenate([class_ref[...].astype(jnp.float32)] * (PAD // samples), axis=0)
     summed = matmul(time_hidden, tout_ref[...]) + jnp.concatenate([classes] * n, axis=0)
     condition = jax.nn.silu(summed).astype(jnp.bfloat16)
-    columns = modw_ref.shape[1]
-    mods_send[...] = matmul(condition, modw_ref[...]).reshape(n, PAD, columns)
+    block, last = modw_ref.shape[0], finalw_ref.shape[0]
+    columns = block + last
+    pieces = [matmul_turned(condition, modw_ref[...]), matmul_turned(condition, finalw_ref[...])]
+    mods_send[...] = jnp.concatenate(pieces, axis=1).reshape(n, PAD, columns)
     mods_recv[me] = mods_send[me]
     for off in range(1, n):
         peer = lax.rem(me + off, n)
         send(mods_send.at[peer], mods_recv.at[me], mods_sems.at[0], mods_sems.at[1], {"tm": peer}).start()
 
-    begin(1)
-    tokens = noise_ref.shape[1]
+    tokens = noise_ref.shape[0]
     per = tokens // samples
 
     current_t, following_t = plan_ref[first + me], plan_ref[first + me + 1]
@@ -408,8 +427,6 @@
             copy.wait_send() if way == 0 else copy.wait_recv()
         flat = mods_recv[...].reshape(n * PAD, columns)
         turned = jnp.transpose(flat).astype(jnp.bfloat16)
-        block = columns * 3 // 4
-        last = columns - block
         row = lax.broadcasted_iota(jnp.int32, (n * PAD, tokens), 0)
         wanted = lax.broadcasted_iota(jnp.int32, (n * PAD, tokens), 1) // per
         for d in range(n):
@@ -437,7 +454,7 @@
 
     def embed(states):
         pos2 = jnp.concatenate([pos_ref[...]] * (tokens // pos_ref.shape[1]), axis=1)
-        hidden[...] = matmul(patch_ref[...], states.astype(jnp.bfloat16)) + pos2
+        hidden[...] = turned_matmul(patch_ref[...], states.astype(jnp.bfloat16)) + pos2
 
     def project():
         normed = normal(0, 1)
@@ -520,13 +537,13 @@
         before = jnp.zeros_like(drift)
         for i in range(PLANE - 1):
             before = before + jnp.where(i < spot, pieces[i], 0.0)
-        out_ref[...] = before
+        before_ref[...] = before
         for b in range(planes - 1):
             @pl.when(b < plane)
             def _():
                 slot = total_recv.at[sweep, b]
                 send(slot, slot, total_ssem.at[sweep, b], total_rsem.at[sweep, b], mate).wait_recv()
-                out_ref[...] += total_recv[sweep, b].astype(jnp.float32)
+                before_ref[...] += total_recv[sweep, b].astype(jnp.float32)
 
         send(some, some, plane_sems.at[sweep, 0], plane_sems.at[sweep, 1], mate).wait_send()
         for b in range(1, planes):
@@ -535,30 +552,54 @@
                 slot = total_send.at[sweep]
                 send(slot, slot, total_ssem.at[sweep, b], total_rsem.at[sweep, 0], mate).wait_send()
 
-        return out_ref[...]
-
-    def arrive(m):
-        for hop in range(1, half + 1):
-            take(m, hop)
-            if hop > 1:
-                take_across(m, hop - 1)
-        take_across(m, half)
-        settle(m)
-
-    noise = noise_ref[...]
+        return before_ref[...]
+
+    noise = jnp.transpose(noise_ref[...])
     states = noise
+    for m in range(3):
+        take(m, 1)
     embed(states)
-    begin(2)
     spread_terms()
-    arrive(0)
-    begin(3)
+    take(3, 1, False)
+    for m in range(4):
+        take_across(m, 1)
+    for hop in range(2, half):
+        take(0, hop)
+        take(1, hop)
+        if hop == 2:
+            onward(3, 1)
+            take(2, 2, False)
+        if hop == 3:
+            onward(2, 2)
+            take(3, 2)
+        if hop > 2:
+            take_across(0, hop - 1)
+            take_across(1, hop - 1)
+    take(0, half)
+    take(1, half)
+    for m in range(2):
+        for hop in range(half - 1, half + 1):
+            take_across(m, hop)
+    settle(0)
     project()
     attend()
-    arrive(1)
+    settle(1)
     mix()
-    arrive(2)
+    take_across(2, 2)
+    take_across(3, 2)
+    for hop in range(3, half):
+        take(2, hop)
+        take(3, hop)
+        take_across(2, hop)
+    take(2, half)
+    for hop in range(3, half):
+        take_across(3, hop)
+    take_across(2, half)
+    settle(2)
     expand()
-    arrive(3)
+    take(3, half)
+    take_across(3, half)
+    settle(3)
     shrink()
     drift = drift_of(states)
     states = noise + earlier(0, drift)
@@ -574,7 +615,7 @@
         drift = drift_of(states)
         before = earlier(sweep, drift)
         states = noise + before
-    out_ref[...] = states + drift
+    out_ref[...] = jnp.transpose(states + drift)
 
 
 def fused_body(
@@ -600,11 +641,8 @@
     count = latent // patch
     tokens = samples * count
     hidden_units = shrink_weight.shape[1]
-    noise_columns = noise.reshape(tokens, patch).T
-    classes = jnp.take(class_table, labels, axis=0, mode="clip")
-    classes = jnp.concatenate([classes] * (PAD // samples), axis=0)
-    modulation = jnp.concatenate([block_modulation[0], final_modulation], axis=1)
-    columns = modulation.shape[1]
+    noise_rows = noise.reshape(tokens, patch)
+    columns = block_modulation.shape[2] + final_modulation.shape[1]
     shards = [w[0].T for w in (query_key_value, mix_weight, expand_weight, shrink_weight)]
     table = position_columns(count, width)
     positions = np.concatenate([table] * (128 // count), axis=1)
@@ -614,8 +652,8 @@
     bf16, f32 = jnp.bfloat16, jnp.float32
     out = pl.pallas_call(
         functools.partial(kernel, n, samples),
-        out_shape=jax.ShapeDtypeStruct((patch, tokens), f32),
-        in_specs=[smem] * 3 + [vmem] * 12,
+        out_shape=jax.ShapeDtypeStruct((tokens, patch), f32),
+        in_specs=[smem] * 3 + [vmem] * 13,
         out_specs=vmem,
         scratch_shapes=[pltpu.VMEM((s.shape[0] * n, s.shape[1]), bf16) for s in shards]
         + [
@@ -641,6 +679,7 @@
             dma((ITERS, 2)),
             dma((ITERS, n // PLANE)),
             dma((ITERS, n // PLANE)),
+            pltpu.VMEM((patch, tokens), f32),
         ],
         compiler_params=pltpu.CompilerParams(
             collective_id=0, has_side_effects=True, vmem_limit_bytes=60 * 1024 * 1024
@@ -649,17 +688,18 @@
         timesteps,
         window_start,
         jnp.asarray(alpha_table()),
-        noise_columns,
-        classes,
+        noise_rows,
+        jnp.take(class_table, labels, axis=0, mode="clip"),
         time_weight_in,
         time_weight_out,
-        modulation,
-        patch_weight.T,
+        block_modulation[0].T,
+        final_modulation.T,
+        patch_weight,
         output_weight.T,
         jnp.asarray(positions),
         *shards,
     )
-    return out.T.reshape(1, samples, latent)
+    return out.reshape(1, samples, latent)
 
 
 def fits(n, groups, args):
@@ -670,6 +710,7 @@
     return (
         groups % 2 == 0
         and n % 8 == 0
+        and n >= 16
         and all(r % 48 == 0 for r in rows)
         and columns % 128 == 0
         and PAD % samples == 0

time: 138 us -> 118 us (0.86)
  Pallas kernels: 129 us -> 111 us
  local copies, waits for them, and re-layouts: 6.46 us -> 4.42 us
    pallas_call x1, Pallas kernels: 129 us -> 111 us  [fused_body(): pl.pallas_call(functools.partial(kernel, n, samples), out_shape=jax.Shape...]
    unnamed x11 -> x2, local copies, waits for them, and re-layouts: 3.38 us -> 0.01 us
    reshape x3 -> x2, local copies, waits for them, and re-layouts: 1.58 us -> 3.26 us  [the longest x1 1.64 us: fused_body(): return out.reshape(1, samples, latent)]
    concatenate x2 -> x0, other arithmetic: 1.56 us -> none  [the longest x1 0.95 us: fused_body(): jnp.concatenate([block_modulation[0], final_modulation], axis=1)]
where the time goes in v2:
time: 118 us; the launch traced here: 117 us
  Pallas kernels  111 us (94%)
  local copies, waits for them, and re-layouts  4.42 us (4%)
    pallas_call x1, Pallas kernels, fused_body(): pl.pallas_call(functools.partial(kernel, n, samples), out_shape=jax.Shape...  111 us

profile of v2, /device:TPU:0, one launch (start us, length us, event | category | flops | bytes accessed | tf_op | source)
XLA Modules:
  0.0 116.7 jit_solution(2452306871882947571)
XLA Ops:
  0.0 0.0 copy-start
  0.8 0.7 pad_clamp_fusion
  1.4 0.0 copy-done
  1.4 1.2 gather_fusion
  2.6 1.6 %reshape.6.noise_ref = f32[256,64]{1,0:T(8,128)} reshape(f32[4,4096]{1,0:T(4,128)} %param.17) | data formatting | bytes 131072 | tf_op jit(solution)/shard_map/reshape | solution.py:644
  4.2 110.9 %shard_map.163 = f32[256,64]{1,0:T(8,128)} custom-call(s32[25]{0:T(128)} %plan_ref.1, s32[1]{0:T(128)S(6)} %copy.18.start_ref, f32[1000]{0:T(1024)} %constant.4.clone.alpha_ref, f32[256,64]{1,0:T(8,128)} %reshape.6.noise_ref, bf16[4,768]{1,0:T(4,128)(2,1)} %gather_fusion, bf16[256,768]{1,0:T(8,128)(2,1)} %tin_ref.1, bf16[768,768]{1,0:T(8,128)(2,1)} %tout_ref.1, ...), custom_call_target="tpu_custom_call" | custom-call | tf_op jit(solution)/shard_map/pallas_call | solution.py:653
  115.1 1.6 %reshape.7 = f32[1,4,4096]{2,1,0:T(4,128)} reshape(f32[256,64]{1,0:T(8,128)} %shard_map.163) | data formatting | bytes 131072 | tf_op jit(solution)/shard_map/reshape | solution.py:702
Async XLA Ops:
  0.0 1.4 %copy-start = (bf16[1001,768]{1,0:T(8,128)(2,1)S(1)}, bf16[1001,768]{1,0:T(8,128)(2,1)}, u32[]{:S(2)}) copy-start(bf16[1001,768]{1,0:T(8,128)(2,1)} %param.23) | copy-start | bytes 4612612

commit v3 on v2

--- a/solution.py
+++ b/solution.py
@@ -386,6 +386,8 @@
 
     for m in range(4):
         begin(m)
+    take(0, 1)
+    take(1, 1)
 
     width = tin_ref.shape[1]
     freq = tin_ref.shape[0]
@@ -450,7 +452,7 @@
             action(pl.ds(pl.multiple_of(i * ROW_TILE, ROW_TILE), ROW_TILE), i)
             return 0
 
-        lax.fori_loop(0, count // ROW_TILE, step, 0)
+        lax.fori_loop(0, count // ROW_TILE, step, 0, unroll=3)
 
     def embed(states):
         pos2 = jnp.concatenate([pos_ref[...]] * (tokens // pos_ref.shape[1]), axis=1)
@@ -485,7 +487,7 @@
                 attended[pl.ds(base, head_dim), cols] = matmul(v, weights).astype(jnp.bfloat16)
             return 0
 
-        lax.fori_loop(0, HEADS, one, 0, unroll=2)
+        lax.fori_loop(0, HEADS, one, 0, unroll=4)
 
     def mix():
         a = attended[...]
@@ -556,11 +558,10 @@
 
     noise = jnp.transpose(noise_ref[...])
     states = noise
-    for m in range(3):
-        take(m, 1)
+    take(2, 1)
     embed(states)
+    take(3, 1, False)
     spread_terms()
-    take(3, 1, False)
     for m in range(4):
         take_across(m, 1)
     for hop in range(2, half):

time: 118 us -> 109 us (0.924)
  Pallas kernels: 111 us -> 102 us
    pallas_call x1, Pallas kernels: 111 us -> 102 us  [fused_body(): pl.pallas_call(functools.partial(kernel, n, samples), out_shape=jax.Shape...]
where the time goes in v3:
time: 109 us; the launch traced here: 108 us
  Pallas kernels  102 us (94%)
  local copies, waits for them, and re-layouts  4.42 us (4%)
    pallas_call x1, Pallas kernels, fused_body(): pl.pallas_call(functools.partial(kernel, n, samples), out_shape=jax.Shape...  102 us

profile of v3, /device:TPU:0, one launch (start us, length us, event | category | flops | bytes accessed | tf_op | source)
XLA Modules:
  0.0 107.8 jit_solution(1349786352286734638)
XLA Ops:
  0.0 0.0 copy-start
  0.8 0.7 pad_clamp_fusion
  1.4 0.0 copy-done
  1.4 1.2 %gather_fusion = bf16[4,768]{1,0:T(4,128)(2,1)} fusion(bf16[1001,768]{1,0:T(8,128)(2,1)S(1)} %copy-done, s32[1024]{0:T(1024)S(1)} %pad_clamp_fusion), kind=kCustom, calls=%fused_computation | custom fusion | bytes 12304 | tf_op jit(solution)/shard_map/jit(_take)/gather | solution.py:693
  2.6 1.6 %reshape.6.noise_ref = f32[256,64]{1,0:T(8,128)} reshape(f32[4,4096]{1,0:T(4,128)} %param.17) | data formatting | bytes 131072 | tf_op jit(solution)/shard_map/reshape | solution.py:645
  4.2 102.0 %shard_map.163 = f32[256,64]{1,0:T(8,128)} custom-call(s32[25]{0:T(128)} %plan_ref.1, s32[1]{0:T(128)S(6)} %copy.18.start_ref, f32[1000]{0:T(1024)} %constant.4.clone.alpha_ref, f32[256,64]{1,0:T(8,128)} %reshape.6.noise_ref, bf16[4,768]{1,0:T(4,128)(2,1)} %gather_fusion, bf16[256,768]{1,0:T(8,128)(2,1)} %tin_ref.1, bf16[768,768]{1,0:T(8,128)(2,1)} %tout_ref.1, ...), custom_call_target="tpu_custom_call" | custom-call | tf_op jit(solution)/shard_map/pallas_call | solution.py:654
  106.2 1.6 %reshape.7 = f32[1,4,4096]{2,1,0:T(4,128)} reshape(f32[256,64]{1,0:T(8,128)} %shard_map.163) | data formatting | bytes 131072 | tf_op jit(solution)/shard_map/reshape | solution.py:703
Async XLA Ops:
  0.0 1.4 %copy-start = (bf16[1001,768]{1,0:T(8,128)(2,1)S(1)}, bf16[1001,768]{1,0:T(8,128)(2,1)}, u32[]{:S(2)}) copy-start(bf16[1001,768]{1,0:T(8,128)(2,1)} %param.23) | copy-start | bytes 4612612
